TPU v7x, 128 devices: a whole 4x4x4 slice. The times are simulated.
128 devices in a mesh: gx: 32 (over y, z, core), gy: 4 (over x).
Axes of the slice: x: 4, y: 4, z: 4, core: 2. Of those that a mesh axis runs over, the one named last changes fastest.
Arguments:
- hamiltonian: bfloat16 [128, 16, 64, 576], P('gx', 'gy'), as said below
- density: bfloat16 [128, 16, 64, 576], P('gx', 'gy'), as said below
- block_pattern: int32 [128, 16, 9], P('gx', 'gy'), may hold values from 0 to 1, as said below
- filter_mask: int32 [128, 16, 9], P('gx', 'gy'), may hold values from 0 to 1, as said below
Outputs:
- gradient: bfloat16 [128, 16, 64, 576], P('gx', 'gy')
Inputs may be any that keep to these rules, and one draw needn't show every extreme that they name: `block_pattern`: Symmetric: the value at block row i and slot k equals the value at block row i + s_k and slot 8 - k; the middle slot (k = 4) is always 1. `filter_mask`: Symmetric: the value at block row i and slot k equals the value at block row i + s_k and slot 8 - k; the middle slot (k = 4) is always 1. `hamiltonian`: A symmetric matrix: block (i, k) is the transpose of block (i + s_k, 8 - k), and every middle block (k = 4) is symmetric. `density`: A symmetric matrix: block (i, k) is the transpose of block (i + s_k, 8 - k), and every middle block (k = 4) is symmetric.
All inputs are finite; a program needn't handle non-finite values.
Results may differ from a plain program's by a relative error of at most 0.006.
Values may be sent and summed in bfloat16 or wider, within the bound.
A program may use at most 192 MiB of HBM per device.

v0:
```python
import jax
import jax.numpy as jnp
import numpy as np
from jax import lax
from jax.sharding import PartitionSpec as P


def with_halo(block, sides, width):
    for axis, dim in sides:
        count = lax.axis_size(axis)
        forward = [(i, i + 1) for i in range(count - 1)]
        forward.append((count - 1, 0))
        backward = [(target, source) for source, target in forward]
        low = lax.ppermute(
            lax.slice_in_dim(block, block.shape[dim] - width, None, axis=dim), axis, forward
        )
        high = lax.ppermute(lax.slice_in_dim(block, 0, width, axis=dim), axis, backward)
        block = jnp.concatenate([low, block, high], axis=dim)
    return block


def slot_table():
    table = np.full((9, 9), 9, dtype=np.int32)
    for source in range(9):
        move_x = source // 3 - 1
        move_y = source % 3 - 1
        for target in range(9):
            rest_x = target // 3 - 1 - move_x
            rest_y = target % 3 - 1 - move_y
            if abs(rest_x) <= 1 and abs(rest_y) <= 1:
                table[source, target] = (rest_x + 1) * 3 + rest_y + 1
    return table


def block_mask(strips, mask, width):
    shape = strips.shape
    split = strips.reshape(shape[0], shape[1], width, 9, width)
    split = split * mask[:, :, None, :, None].astype(strips.dtype)
    return split.reshape(shape)


def stencil_product(left, right, margin, width):
    rows_x = left.shape[0]
    rows_y = left.shape[1]
    table = slot_table()
    stacked = []
    for source in range(9):
        move_x = source // 3 - 1
        move_y = source % 3 - 1
        moved = right[
            margin + move_x : margin + move_x + rows_x, margin + move_y : margin + move_y + rows_y
        ]
        split = moved.reshape(rows_x, rows_y, width, 9, width)
        padded = jnp.concatenate(
            [split, jnp.zeros((rows_x, rows_y, width, 1, width), split.dtype)], axis=3
        )
        stacked.append(jnp.take(padded, jnp.asarray(table[source]), axis=3))
    operand = jnp.stack(stacked, axis=2).reshape(rows_x, rows_y, 9 * width, 9 * width)
    return jnp.einsum("xyak,xykf->xyaf", left, operand, preferred_element_type=jnp.float32)


def transposed(padded, rows_x, rows_y, width):
    blocks = []
    for target in range(9):
        move_x = target // 3 - 1
        move_y = target % 3 - 1
        moved = padded[1 + move_x : 1 + move_x + rows_x, 1 + move_y : 1 + move_y + rows_y]
        blocks.append(moved[:, :, :, (8 - target) * width : (9 - target) * width])
    joined = jnp.stack(blocks, axis=3)
    return jnp.swapaxes(joined, 2, 4).reshape(rows_x, rows_y, width, 9 * width)


def per_device(hamiltonian, density, block_pattern, filter_mask):
    width = hamiltonian.shape[2]
    rows_x = hamiltonian.shape[0]
    rows_y = hamiltonian.shape[1]
    ham_masked = block_mask(hamiltonian, block_pattern, width)
    dens_masked = block_mask(density, block_pattern, width)
    depth = 1
    dens_pad = with_halo(dens_masked, (("gx", 0), ("gy", 1)), depth)
    hpp_pad = None
    hp = block_mask(stencil_product(ham_masked, dens_pad, 1, width), filter_mask, width).astype(
        jnp.bfloat16
    )
    hp_pad = with_halo(hp, (("gx", 0), ("gy", 1)), 1)
    hpp = block_mask(stencil_product(hp, dens_pad, 1, width), filter_mask, width).astype(
        jnp.bfloat16
    )
    php = block_mask(stencil_product(dens_masked, hp_pad, 1, width), filter_mask, width)
    hp_turned = transposed(hp_pad, rows_x, rows_y, width)
    hpp_pad = with_halo(hpp, (("gx", 0), ("gy", 1)), 1)
    hpp_turned = transposed(hpp_pad, rows_x, rows_y, width)
    linear = hp.astype(jnp.float32) + hp_turned.astype(jnp.float32)
    cubic = hpp.astype(jnp.float32) + php + hpp_turned.astype(jnp.float32)
    total = block_mask(3.0 * linear - 2.0 * cubic, filter_mask, width)
    return total.astype(jnp.bfloat16)


def solution(mesh):
    return jax.shard_map(
        per_device,
        mesh=mesh,
        in_specs=(
            P("gx", "gy", None, None),
            P("gx", "gy", None, None),
            P("gx", "gy", None),
            P("gx", "gy", None),
        ),
        out_specs=P("gx", "gy", None, None),
        check_vma=False,
    )
```

profile of v0, /device:TPU:0, one launch (start us, length us, event | category | flops | bytes accessed | tf_op | source)
XLA Modules:
  0.0 543.6 jit_solution(6687401439917762989)
XLA Ops:
  9.8 6.0 %collective-permute-start.1 = (bf16[1,4,64,576]{3,2,1,0:T(8,128)(2,1)}, bf16[1,4,64,576]{3,2,1,0:T(8,128)(2,1)S(1)}, u32[]{:S(2)}, u32[]{:S(2)}) collective-permute-start(bf16[1,4,64,576]{3,2,1,0:T(8,128)(2,1)} %copy.129), channel_id=1, source_target_pairs={{4,0},{8,4},{12,8},{16,12},{20,16},{24,20},{28,24},{32,28},{36,32}... | collective-permute-start | bytes 884744 | tf_op jit(solution)/shard_map/ppermute | solution.py:17
  20.7 6.4 %collective-permute-done = bf16[1,4,64,576]{3,2,1,0:T(8,128)(2,1)S(1)} collective-permute-done((bf16[1,4,64,576]{3,2,1,0:T(8,128)(2,1)}, bf16[1,4,64,576]{3,2,1,0:T(8,128)(2,1)S(1)}, u32[]{:S(2)}, u32[]{:S(2)}) %collective-permute-start) | collective-permute-done | bytes 294944 | tf_op jit(solution)/shard_map/ppermute | solution.py:14
  43.0 4.3 copy.133
  53.8 4.3 copy.143
  144.8 4.3 gather_fusion.5
  164.8 25.1 %copy.146 = bf16[4,4,9,64,9,64]{5,4,3,2,1,0:T(8,128)(2,1)} copy(bf16[4,4,9,64,9,64]{5,3,1,0,4,2:T(8,128)(2,1)} %bitcast_dynamic-update-slice_fusion.9) | data formatting | bytes 21233664 | tf_op jit(solution)/shard_map/stack | solution.py:58
  190.0 42.4 %reshape.114 = bf16[4,4,576,576]{3,2,1,0:T(8,128)(2,1)} reshape(bf16[4,4,9,64,9,64]{5,4,3,2,1,0:T(8,128)(2,1)} %copy.146) | data formatting | bytes 21233664 | tf_op jit(solution)/shard_map/reshape | solution.py:58
  232.3 6.8 %multiply_convert_fusion.2 = (bf16[4,4,64,576]{3,2,1,0:T(8,128)(2,1)S(1)}, f32[4,4,64,576]{3,2,1,0:T(8,128)S(1)}) fusion(f32[4,4,576]{2,1,0:T(4,128)S(1)} %mul.78, bf16[4,4,576,576]{3,2,1,0:T(8,128)(2,1)} %reshape.114, bf16[4,4,64,576]{3,2,1,0:T(8,128)(2,1)S(1)} %copy-done.24, bf16[4,4,576]{2,1,0:T(4,128)(2,1)S(1)} %mul.71), kind=kOutput, calls=%fused_computation.22 | convolution fusion | flops 681246720 | bytes 15390720 | tf_op jit(solution)/shard_map/xyak,xykf->xyaf/dot_general | solution.py:59
  243.8 4.6 collective-permute-start.5
  256.7 4.3 copy.158
  281.7 4.3 copy.152
  297.9 4.3 copy.164
  320.4 5.1 copy.169
  335.3 5.0 copy.148
  349.2 4.3 copy.150
  371.4 4.5 copy.154
  387.7 4.3 copy.156
  403.9 4.3 copy.160
  418.8 4.3 copy.162
  427.1 4.3 gather_fusion.15
  433.9 4.5 copy.166
  465.7 25.1 %copy.167 = bf16[4,4,9,64,9,64]{5,4,3,2,1,0:T(8,128)(2,1)} copy(bf16[4,4,9,64,9,64]{5,3,1,0,4,2:T(8,128)(2,1)} %bitcast_dynamic-update-slice_fusion) | data formatting | bytes 21233664 | tf_op jit(solution)/shard_map/stack | solution.py:58
  490.8 42.4 %reshape.125 = bf16[4,4,576,576]{3,2,1,0:T(8,128)(2,1)} reshape(bf16[4,4,9,64,9,64]{5,4,3,2,1,0:T(8,128)(2,1)} %copy.167) | data formatting | bytes 21233664 | tf_op jit(solution)/shard_map/reshape | solution.py:58
  533.2 10.2 %multiply_convert_fusion = bf16[4,4,64,576]{3,2,1,0:T(8,128)(2,1)} fusion(f32[4,4,64,576]{3,2,1,0:T(8,128)} %copy.169, bf16[4,4,64,576]{3,2,1,0:T(8,128)(2,1)S(1)} %multiply_convert_fusion.1, f32[4,4,64,576]{3,2,1,0:T(8,128)} %copy.148, f32[4,4,64,576]{3,2,1,0:T(8,128)} %copy-done.3, bf16[4,4,64,576]{3,2,1,0:T(8,128)(2,1)S(1)} %copy-done.2, ...), kind=kOutput, calls=%fused_computation.20 | convolution fusion | flops 687144960 | bytes 21270528 | tf_op jit(solution)/shard_map/xyak,xykf->xyaf/dot_general | solution.py:59
  (223 shorter events, 307.1 us)
Async XLA Ops:
  8.5 8.6 %copy-start.32 = (s32[9]{0:T(128)S(1)}, s32[9]{0:T(128)}, u32[]{:S(2)}) copy-start(s32[9]{0:T(128)} %constant.228) | copy-start | bytes 112
  8.5 8.6 %copy-start.34 = (s32[9]{0:T(128)S(1)}, s32[9]{0:T(128)}, u32[]{:S(2)}) copy-start(s32[9]{0:T(128)} %constant.227) | copy-start | bytes 112
  8.5 8.6 %copy-start.33 = (s32[9]{0:T(128)S(1)}, s32[9]{0:T(128)}, u32[]{:S(2)}) copy-start(s32[9]{0:T(128)} %constant.229) | copy-start | bytes 112
  8.5 8.6 %copy-start.31 = (s32[9]{0:T(128)S(1)}, s32[9]{0:T(128)}, u32[]{:S(2)}) copy-start(s32[9]{0:T(128)} %constant.226) | copy-start | bytes 112
  8.5 8.9 %copy-start.22 = (bf16[4,4,64,576]{3,2,1,0:T(8,128)(2,1)S(1)}, bf16[4,4,64,576]{3,2,1,0:T(8,128)(2,1)}, u32[]{:S(2)}) copy-start(bf16[4,4,64,576]{3,2,1,0:T(8,128)(2,1)} %param.34) | copy-start | bytes 3538948
  9.8 10.9 %collective-permute-start.1 = (bf16[1,4,64,576]{3,2,1,0:T(8,128)(2,1)}, bf16[1,4,64,576]{3,2,1,0:T(8,128)(2,1)S(1)}, u32[]{:S(2)}, u32[]{:S(2)}) collective-permute-start(bf16[1,4,64,576]{3,2,1,0:T(8,128)(2,1)} %copy.129), channel_id=1, source_target_pairs={{4,0},{8,4},{12,8},{16,12},{20,16},{24,20},{28,24},{32,28},{36,32}... | collective-permute-start | bytes 884744 | tf_op jit(solution)/shard_map/ppermute | solution.py:17
  17.1 10.0 %collective-permute-start = (bf16[1,4,64,576]{3,2,1,0:T(8,128)(2,1)}, bf16[1,4,64,576]{3,2,1,0:T(8,128)(2,1)S(1)}, u32[]{:S(2)}, u32[]{:S(2)}) collective-permute-start(bf16[1,4,64,576]{3,2,1,0:T(8,128)(2,1)} %copy.127), channel_id=1, source_target_pairs={{0,4},{4,8},{8,12},{12,16},{16,20},{20,24},{24,28},{28,32},{32,36}... | collective-permute-start | bytes 884744 | tf_op jit(solution)/shard_map/ppermute | solution.py:14
  17.4 13.7 %copy-start.21 = (bf16[4,4,64,9,64]{4,2,3,1,0:T(8,128)(2,1)S(1)}, bf16[4,4,64,9,64]{4,2,3,1,0:T(8,128)(2,1)}, u32[]{:S(2)}) copy-start(bf16[4,4,64,9,64]{4,2,3,1,0:T(8,128)(2,1)} %copy-done.20) | copy-start | bytes 3538948
  17.6 53.0 %copy-start.1 = (bf16[4,4,64,576]{3,2,1,0:T(8,128)(2,1)}, bf16[4,4,64,576]{3,2,1,0:T(8,128)(2,1)S(1)}, u32[]{:S(2)}) copy-start(bf16[4,4,64,576]{3,2,1,0:T(8,128)(2,1)S(1)} %broadcast_multiply_fusion.1) | copy-start | bytes 3538948
  28.3 42.3 %collective-permute-start.3 = (bf16[6,1,64,576]{3,2,1,0:T(8,128)(2,1)}, bf16[6,1,64,576]{3,2,1,0:T(8,128)(2,1)}, u32[]{:S(2)}, u32[]{:S(2)}) collective-permute-start(bf16[6,1,64,576]{3,2,1,0:T(8,128)(2,1)} %get-tuple-element.28), channel_id=1, source_target_pairs={{1,0},{2,1},{3,2},{0,3},{5,4},{6,5},{7,6},{4,7},{9,8},{10,9},{11,1... | collective-permute-start | bytes 1327112 | tf_op jit(solution)/shard_map/ppermute | solution.py:17
  31.1 39.5 %collective-permute-start.2 = (bf16[6,1,64,576]{3,2,1,0:T(8,128)(2,1)}, bf16[6,1,64,576]{3,2,1,0:T(8,128)(2,1)}, u32[]{:S(2)}, u32[]{:S(2)}) collective-permute-start(bf16[6,1,64,576]{3,2,1,0:T(8,128)(2,1)} %get-tuple-element.29), channel_id=1, source_target_pairs={{0,1},{1,2},{2,3},{3,0},{4,5},{5,6},{6,7},{7,4},{8,9},{9,10},{10,1... | collective-permute-start | bytes 1327112 | tf_op jit(solution)/shard_map/ppermute | solution.py:14
  144.8 4.4 copy-start.10
  190.0 42.4 %copy-start.24 = (bf16[4,4,64,576]{3,2,1,0:T(8,128)(2,1)S(1)}, bf16[4,4,64,576]{3,2,1,0:T(8,128)(2,1)}, u32[]{:S(2)}) copy-start(bf16[4,4,64,576]{3,2,1,0:T(8,128)(2,1)} %param.33) | copy-start | bytes 3538948
  232.3 7.7 %copy-start = (bf16[4,4,576,576]{3,2,1,0:T(8,128)(2,1)S(1)}, bf16[4,4,576,576]{3,2,1,0:T(8,128)(2,1)}, u32[]{:S(2)}) copy-start(bf16[4,4,576,576]{3,2,1,0:T(8,128)(2,1)} %reshape.114) | copy-start | bytes 31850500
  242.3 6.1 %collective-permute-start.9 = (bf16[1,4,64,576]{3,2,1,0:T(8,128)(2,1)S(1)}, bf16[1,4,64,576]{3,2,1,0:T(8,128)(2,1)S(1)}, u32[]{:S(2)}, u32[]{:S(2)}) collective-permute-start(bf16[1,4,64,576]{3,2,1,0:T(8,128)(2,1)S(1)} %get-tuple-element.35), channel_id=1, source_target_pairs={{4,0},{8,4},{12,8},{16,12},{20,16},{24,20},{28,24},{32,28},{36,32}... | collective-permute-start | bytes 884744 | tf_op jit(solution)/shard_map/ppermute | solution.py:17
  242.4 9.9 %collective-permute-start.8 = (bf16[1,4,64,576]{3,2,1,0:T(8,128)(2,1)S(1)}, bf16[1,4,64,576]{3,2,1,0:T(8,128)(2,1)S(1)}, u32[]{:S(2)}, u32[]{:S(2)}) collective-permute-start(bf16[1,4,64,576]{3,2,1,0:T(8,128)(2,1)S(1)} %get-tuple-element.34), channel_id=1, source_target_pairs={{0,4},{4,8},{8,12},{12,16},{16,20},{20,24},{24,28},{28,32},{32,36}... | collective-permute-start | bytes 884744 | tf_op jit(solution)/shard_map/ppermute | solution.py:14
  243.8 27.9 %collective-permute-start.5 = (bf16[1,4,64,576]{3,2,1,0:T(8,128)(2,1)}, bf16[1,4,64,576]{3,2,1,0:T(8,128)(2,1)S(1)}, u32[]{:S(2)}, u32[]{:S(2)}) collective-permute-start(bf16[1,4,64,576]{3,2,1,0:T(8,128)(2,1)} %get-tuple-element.33), channel_id=1, source_target_pairs={{4,0},{8,4},{12,8},{16,12},{20,16},{24,20},{28,24},{32,28},{36,32}... | collective-permute-start | bytes 884744 | tf_op jit(solution)/shard_map/ppermute | solution.py:17
  248.4 23.2 %collective-permute-start.4 = (bf16[1,4,64,576]{3,2,1,0:T(8,128)(2,1)}, bf16[1,4,64,576]{3,2,1,0:T(8,128)(2,1)S(1)}, u32[]{:S(2)}, u32[]{:S(2)}) collective-permute-start(bf16[1,4,64,576]{3,2,1,0:T(8,128)(2,1)} %get-tuple-element.32), channel_id=1, source_target_pairs={{0,4},{4,8},{8,12},{12,16},{16,20},{20,24},{24,28},{28,32},{32,36}... | collective-permute-start | bytes 884744 | tf_op jit(solution)/shard_map/ppermute | solution.py:14
  253.5 57.0 %collective-permute-start.10 = (bf16[6,1,64,576]{3,2,1,0:T(8,128)(2,1)}, bf16[6,1,64,576]{3,2,1,0:T(8,128)(2,1)}, u32[]{:S(2)}, u32[]{:S(2)}) collective-permute-start(bf16[6,1,64,576]{3,2,1,0:T(8,128)(2,1)} %get-tuple-element.25), channel_id=1, source_target_pairs={{0,1},{1,2},{2,3},{3,0},{4,5},{5,6},{6,7},{7,4},{8,9},{9,10},{10,1... | collective-permute-start | bytes 1327112 | tf_op jit(solution)/shard_map/ppermute | solution.py:14
  269.2 42.5 %collective-permute-start.11 = (bf16[6,1,64,576]{3,2,1,0:T(8,128)(2,1)}, bf16[6,1,64,576]{3,2,1,0:T(8,128)(2,1)}, u32[]{:S(2)}, u32[]{:S(2)}) collective-permute-start(bf16[6,1,64,576]{3,2,1,0:T(8,128)(2,1)} %get-tuple-element.24), channel_id=1, source_target_pairs={{1,0},{2,1},{3,2},{0,3},{5,4},{6,5},{7,6},{4,7},{9,8},{10,9},{11,1... | collective-permute-start | bytes 1327112 | tf_op jit(solution)/shard_map/ppermute | solution.py:17
  272.8 52.7 %collective-permute-start.6 = (bf16[6,1,64,576]{3,2,1,0:T(8,128)(2,1)}, bf16[6,1,64,576]{3,2,1,0:T(8,128)(2,1)}, u32[]{:S(2)}, u32[]{:S(2)}) collective-permute-start(bf16[6,1,64,576]{3,2,1,0:T(8,128)(2,1)} %get-tuple-element.23), channel_id=1, source_target_pairs={{0,1},{1,2},{2,3},{3,0},{4,5},{5,6},{6,7},{7,4},{8,9},{9,10},{10,1... | collective-permute-start | bytes 1327112 | tf_op jit(solution)/shard_map/ppermute | solution.py:14
  272.8 53.8 %collective-permute-start.7 = (bf16[6,1,64,576]{3,2,1,0:T(8,128)(2,1)}, bf16[6,1,64,576]{3,2,1,0:T(8,128)(2,1)}, u32[]{:S(2)}, u32[]{:S(2)}) collective-permute-start(bf16[6,1,64,576]{3,2,1,0:T(8,128)(2,1)} %get-tuple-element.22), channel_id=1, source_target_pairs={{1,0},{2,1},{3,2},{0,3},{5,4},{6,5},{7,6},{4,7},{9,8},{10,9},{11,1... | collective-permute-start | bytes 1327112 | tf_op jit(solution)/shard_map/ppermute | solution.py:17
  427.1 4.3 copy-start.23
  490.8 42.4 %copy-start.2 = (bf16[4,4,64,576]{3,2,1,0:T(8,128)(2,1)S(1)}, bf16[4,4,64,576]{3,2,1,0:T(8,128)(2,1)}, u32[]{:S(2)}) copy-start(bf16[4,4,64,576]{3,2,1,0:T(8,128)(2,1)} %copy-done.1) | copy-start | bytes 3538948
  (23 other events, 61.7 us)
where the time goes:
time: 554 us; the launch traced here: 544 us
  local copies, waits for them, and re-layouts  459 us (83%)
  other arithmetic  30.4 us (5%)
  starting transfers between devices  20.5 us (4%)
  matrix products  19.1 us (3%)
  waiting for transfers between devices  13.4 us (2%)
    reshape x2, local copies, waits for them, and re-layouts, stencil_product(): jnp.stack(stacked, axis=2).reshape(rows_x, rows_y, 9 * width, 9 * width)  84.7 us
    gather x18, local copies, waits for them, and re-layouts, stencil_product(): stacked.append(jnp.take(padded, jnp.asarray(table[source]), axis=3))  68.3 us
    reshape x17, local copies, waits for them, and re-layouts, stencil_product(): split = moved.reshape(rows_x, rows_y, width, 9, width)  65.9 us
    concatenate x18, local copies, waits for them, and re-layouts, stencil_product(): jnp.concatenate([split, jnp.zeros((rows_x, rows_y, width, 1, width), spli...  60.3 us
    another operation x4, local copies, waits for them, and re-layouts, stencil_product(): jnp.stack(stacked, axis=2).reshape(rows_x, rows_y, 9 * width, 9 * width)  54.3 us
    unnamed x87, local copies, waits for them, and re-layouts  39 us
    slice x10, local copies, waits for them, and re-layouts, transposed(): padded[1 + move_x:1 + move_x + rows_x, 1 + move_y:1 + move_y + rows_y]  31.2 us
    slice x9, local copies, waits for them, and re-layouts, stencil_product(): right[margin + move_x:margin + move_x + rows_x, margin + move_y:margin +...  30.1 us
  transfers between devices with their start and end apart: 12, of which 3 were waited for; matrix products, arithmetic and copies ran while one was open for 20% of the time, Pallas kernels for 0%

commit v1 on v0

v1 whole, which is shorter than its diff:
```python
import functools

import jax
import jax.numpy as jnp
from jax import lax
from jax.experimental import pallas as pl
from jax.experimental.pallas import tpu as pltpu
from jax.sharding import PartitionSpec as P

TILE = 256
LANES = 3 * TILE
MESH = pl.DeviceIdType.MESH
SIDES = ((1, 0), (-1, 0), (0, 1), (0, -1), (1, 1), (1, -1), (-1, 1), (-1, -1))


def halo_parts(sx, sy):
    from_x = {1: pl.ds(4, 1), -1: pl.ds(1, 1), 0: pl.ds(1, 4)}[sx]
    to_x = {1: pl.ds(0, 1), -1: pl.ds(5, 1), 0: pl.ds(1, 4)}[sx]
    from_y = {1: pl.ds(4, 1), -1: pl.ds(1, 1), 0: pl.ds(1, 4)}[sy]
    to_y = {1: pl.ds(0, 1), -1: pl.ds(5, 1), 0: pl.ds(1, 4)}[sy]
    tiles = {1: (1, 2), -1: (0, 1), 0: (0, 1, 2)}[sx]
    if sy == 0:
        lanes = [(TILE * tiles[0], TILE * len(tiles))]
    else:
        lanes = [(TILE * t + (128 if sy == 1 else 0), 128) for t in tiles]
    return [
        ((from_x, from_y, slice(None), pl.ds(start, size)), (to_x, to_y, slice(None), pl.ds(start, size)))
        for start, size in lanes
    ]


COPIES = sum(len(halo_parts(sx, sy)) for sx, sy in SIDES)


def kernel(
    nx, ny, ham, den, pat, fil, out,
    raw_h, raw_d, pat_row, fil_row, e_h, e_d, e_s, hp, total, result,
    load_sem, store_sem, send_sem, recv_sem,
):
    gx = lax.axis_index("gx")
    gy = lax.axis_index("gy")

    def device(sx, sy):
        return (lax.rem(gx + (sx + nx), nx), lax.rem(gy + (sy + ny), ny))

    load_d = pltpu.make_async_copy(den, raw_d, load_sem.at[0])
    load_h = pltpu.make_async_copy(ham, raw_h, load_sem.at[1])
    load_d.start()
    load_h.start()

    barrier = pltpu.get_barrier_semaphore()
    for sx, sy in SIDES:
        pl.semaphore_signal(barrier, inc=1, device_id=device(sx, sy), device_id_type=MESH)

    row = lax.broadcasted_iota(jnp.int32, (4, LANES), 0)
    lane = lax.broadcasted_iota(jnp.int32, (4, LANES), 1)
    place = ((lane >> 6) & 3) - (row & 1)
    slot = jnp.where((place >= 0) & (place <= 2), 3 * (lane >> 8) + place, 9)
    for x in range(4):
        for source, target in ((pat, pat_row), (fil, fil_row)):
            spread = jnp.zeros((4, LANES), jnp.int32)
            for k in range(9):
                spread = jnp.where(slot == k, source[x, :, k : k + 1], spread)
            target[x] = spread.astype(jnp.float32)

    def spread_strips(raw, e):
        def body(step, carry):
            x = step // 2
            p = step % 2
            gap = jnp.zeros((64, 64), jnp.bfloat16)
            v = raw[x, 2 * p]
            m = pat_row[x, pl.ds(2 * p, 1), :].astype(jnp.bfloat16)
            e[x + 1, 2 * p + 1, :, 0:256] = v[:, 0:256] * m[:, 0:256]
            e[x + 1, 2 * p + 1, :, 256:512] = v[:, 192:448] * m[:, 256:512]
            e[x + 1, 2 * p + 1, :, 512:768] = (
                jnp.concatenate([v[:, 384:576], gap], axis=1) * m[:, 512:768]
            )
            v = raw[x, 2 * p + 1]
            m = pat_row[x, pl.ds(2 * p + 1, 1), :].astype(jnp.bfloat16)
            e[x + 1, 2 * p + 2, :, 0:256] = (
                jnp.concatenate([gap, v[:, 0:192]], axis=1) * m[:, 0:256]
            )
            e[x + 1, 2 * p + 2, :, 256:512] = v[:, 128:384] * m[:, 256:512]
            e[x + 1, 2 * p + 2, :, 512:768] = v[:, 320:576] * m[:, 512:768]
            return carry

        lax.fori_loop(0, 8, body, 0)

    def copies(e, base):
        made = []
        for sx, sy in SIDES:
            for source, target in halo_parts(sx, sy):
                made.append(
                    pltpu.make_async_remote_copy(
                        src_ref=e.at[source],
                        dst_ref=e.at[target],
                        send_sem=send_sem.at[base + len(made)],
                        recv_sem=recv_sem.at[base + len(made)],
                        device_id=device(sx, sy),
                        device_id_type=MESH,
                    )
                )
        return made

    copies_d = copies(e_d, 0)
    copies_h = copies(e_h, COPIES)
    copies_s = copies(e_s, 2 * COPIES)

    load_d.wait()
    spread_strips(raw_d, e_d)
    pl.semaphore_wait(barrier, len(SIDES))
    for copy in copies_d:
        copy.start()
    load_h.wait()
    spread_strips(raw_h, e_h)
    for copy in copies_h:
        copy.start()

    hole = jnp.zeros((64, 128), jnp.bfloat16)

    def product(left, e, x, p, target):
        low = max(target - 1, 0)
        high = min(target + 1, 2)
        rights = []
        for source in range(low, high + 1):
            start = TILE * (target - source + 1)
            first = e[x + source, 2 * p, :, start + 128 : start + 256]
            second = e[x + source, 2 * p + 1, :, start : start + 256]
            third = e[x + source, 2 * p + 2, :, start : start + 256]
            fourth = e[x + source, 2 * p + 3, :, start : start + 128]
            rights.append(jnp.concatenate([first, hole], axis=1))
            rights.append(second)
            rights.append(third)
            rights.append(jnp.concatenate([hole, fourth], axis=1))
        a = left[:, :, TILE * low : TILE * (high + 1)]
        a = a.reshape(128, TILE * (high + 1 - low))
        b = jnp.concatenate(rights, axis=0)
        return jnp.dot(a, b, preferred_element_type=jnp.float32)

    def filter_of(x, p, target):
        even = fil_row[x, pl.ds(2 * p, 1), TILE * target : TILE * (target + 1)]
        odd = fil_row[x, pl.ds(2 * p + 1, 1), TILE * target : TILE * (target + 1)]
        return jnp.concatenate(
            [jnp.broadcast_to(even, (64, TILE)), jnp.broadcast_to(odd, (64, TILE))], axis=0
        )

    def pair(step):
        return step // 2, step % 2

    def hp_body(step, carry):
        x, p = pair(step)
        left = e_h[x + 1, pl.ds(2 * p + 1, 2)]
        for target in range(3):
            value = product(left, e_d, x, p, target) * filter_of(x, p, target)
            hp[x, pl.ds(2 * p, 2), :, TILE * target : TILE * (target + 1)] = value.astype(
                jnp.bfloat16
            ).reshape(2, 64, TILE)
        return carry

    def sum_body(step, carry):
        x, p = pair(step)
        left = e_d[x + 1, pl.ds(2 * p + 1, 2)]
        for target in range(3):
            lanes = slice(TILE * target, TILE * (target + 1))
            turned = product(left, e_h, x, p, target) * filter_of(x, p, target)
            turned = turned.astype(jnp.bfloat16).astype(jnp.float32)
            both = turned + hp[x, pl.ds(2 * p, 2), :, lanes].reshape(128, TILE).astype(jnp.float32)
            total[x, pl.ds(2 * p, 2), :, lanes] = (3.0 * both).reshape(2, 64, TILE)
            e_s[x + 1, pl.ds(2 * p + 1, 2), :, lanes] = both.astype(jnp.bfloat16).reshape(
                2, 64, TILE
            )
        return carry

    def hpp_body(step, carry):
        x, p = pair(step)
        left = hp[x, pl.ds(2 * p, 2)]
        for target in range(3):
            lanes = slice(TILE * target, TILE * (target + 1))
            value = product(left, e_d, x, p, target).reshape(2, 64, TILE)
            total[x, pl.ds(2 * p, 2), :, lanes] = (
                total[x, pl.ds(2 * p, 2), :, lanes] - 2.0 * value
            )
        return carry

    def store(x):
        return pltpu.make_async_copy(result.at[x], out.at[x], store_sem.at[x])

    def last_body(x, carry):
        for p in range(2):
            left = e_d[x + 1, pl.ds(2 * p + 1, 2)]
            parts = []
            for target in range(3):
                lanes = slice(TILE * target, TILE * (target + 1))
                value = product(left, e_s, x, p, target)
                value = total[x, pl.ds(2 * p, 2), :, lanes].reshape(128, TILE) - 2.0 * value
                parts.append((value * filter_of(x, p, target)).astype(jnp.bfloat16))
            result[x, 2 * p] = jnp.concatenate([part[0:64, 0:192] for part in parts], axis=1)
            result[x, 2 * p + 1] = jnp.concatenate(
                [part[64:128, 64:256] for part in parts], axis=1
            )
        return carry

    for copy in copies_d:
        copy.wait_recv()
    lax.fori_loop(0, 8, hp_body, 0)
    for copy in copies_h:
        copy.wait_recv()
    lax.fori_loop(0, 8, sum_body, 0)
    for copy in copies_s:
        copy.start()
    lax.fori_loop(0, 8, hpp_body, 0)
    for copy in copies_s:
        copy.wait_recv()
    lax.fori_loop(0, 4, last_body, 0)
    for x in range(4):
        store(x).start()
    for copy in copies_d + copies_h + copies_s:
        copy.wait_send()
    for x in range(4):
        store(x).wait()


def per_device(nx, ny, hamiltonian, density, block_pattern, filter_mask):
    shape = hamiltonian.shape
    ring = (6, 6, 64, LANES)
    vmem = pl.BlockSpec(memory_space=pltpu.VMEM)
    anywhere = pl.BlockSpec(memory_space=pl.ANY)
    return pl.pallas_call(
        functools.partial(kernel, nx, ny),
        out_shape=jax.ShapeDtypeStruct(shape, jnp.bfloat16),
        in_specs=[anywhere, anywhere, vmem, vmem],
        out_specs=anywhere,
        scratch_shapes=[
            pltpu.VMEM(shape, jnp.bfloat16),
            pltpu.VMEM(shape, jnp.bfloat16),
            pltpu.VMEM((4, 4, LANES), jnp.float32),
            pltpu.VMEM((4, 4, LANES), jnp.float32),
            pltpu.VMEM(ring, jnp.bfloat16),
            pltpu.VMEM(ring, jnp.bfloat16),
            pltpu.VMEM(ring, jnp.bfloat16),
            pltpu.VMEM((4, 4, 64, LANES), jnp.bfloat16),
            pltpu.VMEM((4, 4, 64, LANES), jnp.float32),
            pltpu.VMEM(shape, jnp.bfloat16),
            pltpu.SemaphoreType.DMA((2,)),
            pltpu.SemaphoreType.DMA((4,)),
            pltpu.SemaphoreType.DMA((3 * COPIES,)),
            pltpu.SemaphoreType.DMA((3 * COPIES,)),
        ],
        compiler_params=pltpu.CompilerParams(collective_id=0, has_side_effects=True),
    )(hamiltonian, density, block_pattern, filter_mask)


def solution(mesh):
    return jax.shard_map(
        functools.partial(per_device, mesh.shape["gx"], mesh.shape["gy"]),
        mesh=mesh,
        in_specs=(
            P("gx", "gy", None, None),
            P("gx", "gy", None, None),
            P("gx", "gy", None),
            P("gx", "gy", None),
        ),
        out_specs=P("gx", "gy", None, None),
        check_vma=False,
    )
```

time: 554 us -> 38.6 us (0.07); the launches traced: 544 us -> 38.4 us
  local copies, waits for them, and re-layouts: 459 us -> 2.49 us
  Pallas kernels: 0 us -> 35.9 us
  other arithmetic: 30.4 us -> 0 us
  starting transfers between devices: 20.5 us -> 0 us
  matrix products: 19.1 us -> 0 us
  waiting for transfers between devices: 13.4 us -> 0 us
    reshape x20 -> x0, local copies, waits for them, and re-layouts: 154 us -> none  [the longest x2 84.7 us: stencil_product(): jnp.stack(stacked, axis=2).reshape(rows_x, rows_y, 9 * width, 9 * width)]
    gather x18 -> x0, local copies, waits for them, and re-layouts: 68.3 us -> none  [stencil_product(): stacked.append(jnp.take(padded, jnp.asarray(table[source]), axis=3))]
    slice x26 -> x0, local copies, waits for them, and re-layouts: 64.9 us -> none  [the longest x10 31.2 us: transposed(): padded[1 + move_x:1 + move_x + rows_x, 1 + move_y:1 + move_y + rows_y]]
    concatenate x18 -> x0, local copies, waits for them, and re-layouts: 60.3 us -> none  [stencil_product(): jnp.concatenate([split, jnp.zeros((rows_x, rows_y, width, 1, width), spli...]
    another operation x5 -> x0, local copies, waits for them, and re-layouts: 54.3 us -> none  [the longest x4 54.3 us: stencil_product(): jnp.stack(stacked, axis=2).reshape(rows_x, rows_y, 9 * width, 9 * width)]
    unnamed x87 -> x1, local copies, waits for them, and re-layouts: 39 us -> 2.49 us
    pallas_call x0 -> x1, Pallas kernels: none -> 35.9 us  [per_device(): pl.pallas_call(functools.partial(kernel, nx, ny), out_shape=jax.ShapeDtyp...]
    ppermute x12 -> x0, starting transfers between devices: 20.5 us -> none  [the longest x6 19.2 us: with_halo(): lax.ppermute(lax.slice_in_dim(block, 0, width, axis=dim), axis, backward)]
  transfers between devices with their start and end apart: 12 -> 0, of which waited for: 3 -> 0; matrix products, arithmetic and copies ran while one was open for 20% -> 0% of each run, Pallas kernels for 0% -> 0%
where the time goes in v1:
time: 38.6 us; the launch traced here: 38.4 us
  Pallas kernels  35.9 us (93%)
  local copies, waits for them, and re-layouts  2.49 us (6%)
    pallas_call x1, Pallas kernels, per_device(): pl.pallas_call(functools.partial(kernel, nx, ny), out_shape=jax.ShapeDtyp...  35.9 us
    unnamed x1, local copies, waits for them, and re-layouts  2.49 us

profile of v1, /device:TPU:0, one launch (start us, length us, event | category | flops | bytes accessed | tf_op | source)
XLA Modules:
  0.0 38.4 jit_solution(6005391481226754215)
XLA Ops:
  0.0 35.9 %shard_map.46 = bf16[4,4,64,576]{3,2,1,0:T(8,128)(2,1)} custom-call(bf16[4,4,64,576]{3,2,1,0:T(8,128)(2,1)} %ham.1, bf16[4,4,64,576]{3,2,1,0:T(8,128)(2,1)} %den.1, s32[4,4,9]{2,1,0:T(4,128)} %pat.1, s32[4,4,9]{2,1,0:T(4,128)} %fil.1), custom_call_target="tpu_custom_call" | custom-call | tf_op jit(solution)/shard_map/pallas_call | solution.py:228
  35.9 2.5 %copy.6 = bf16[4,4,64,576]{3,2,1,0:T(8,128)(2,1)} copy(bf16[4,4,64,576]{3,2,1,0:T(8,128)(2,1)} %shard_map.46) | data formatting | bytes 2359296

commit v2 on v1

--- a/solution.py
+++ b/solution.py
@@ -10,26 +10,67 @@
 TILE = 256
 LANES = 3 * TILE
 MESH = pl.DeviceIdType.MESH
-SIDES = ((1, 0), (-1, 0), (0, 1), (0, -1), (1, 1), (1, -1), (-1, 1), (-1, -1))
+SIDES = ((1, 1), (1, -1), (-1, 1), (-1, -1), (0, 1), (0, -1), (1, 0), (-1, 0))
 
 
 def halo_parts(sx, sy):
+    whole = slice(None)
     from_x = {1: pl.ds(4, 1), -1: pl.ds(1, 1), 0: pl.ds(1, 4)}[sx]
     to_x = {1: pl.ds(0, 1), -1: pl.ds(5, 1), 0: pl.ds(1, 4)}[sx]
     from_y = {1: pl.ds(4, 1), -1: pl.ds(1, 1), 0: pl.ds(1, 4)}[sy]
     to_y = {1: pl.ds(0, 1), -1: pl.ds(5, 1), 0: pl.ds(1, 4)}[sy]
-    tiles = {1: (1, 2), -1: (0, 1), 0: (0, 1, 2)}[sx]
+    half = 128 if sy == 1 else 0
     if sy == 0:
-        lanes = [(TILE * tiles[0], TILE * len(tiles))]
+        parts = [(from_x, to_x, TILE, TILE)]
+    elif sx != 0:
+        parts = [(from_x, to_x, TILE + half, 128)]
     else:
-        lanes = [(TILE * t + (128 if sy == 1 else 0), 128) for t in tiles]
+        first = pl.ds(1, 1)
+        parts = [
+            (first, first, half, 128),
+            (from_x, to_x, 2 * TILE + half, 128),
+            (from_x, to_x, TILE + half, 128),
+        ]
     return [
-        ((from_x, from_y, slice(None), pl.ds(start, size)), (to_x, to_y, slice(None), pl.ds(start, size)))
-        for start, size in lanes
+        ((a, from_y, whole, pl.ds(start, size)), (b, to_y, whole, pl.ds(start, size)))
+        for a, b, start, size in parts
     ]
 
 
 COPIES = sum(len(halo_parts(sx, sy)) for sx, sy in SIDES)
+
+
+def turn_dense(e, x, y, tile):
+    at = TILE * tile
+    pile = jnp.concatenate([e[x, y, :, at + 128 : at + 256], e[x, y + 1, :, at : at + 128]], axis=0)
+    return pile.T
+
+
+def fill_inner(e):
+    for x, ring, tile in ((1, 0, 0), (4, 5, 2)):
+        here, there = TILE * tile, TILE * (2 - tile)
+        turned = turn_dense(e, x, 2, tile)
+        e[ring, 2, :, there + 128 : there + 256] = turned[0:64]
+        e[ring, 3, :, there : there + 128] = turned[64:128]
+        for y in (2, 4):
+            pile = jnp.concatenate(
+                [e[x, y, :, here : here + 128], e[x, y - 1, :, here + 128 : here + 256]], axis=0
+            )
+            turned = pile.T
+            e[ring, y, :, there : there + 128] = turned[0:64]
+            e[ring, y - 1, :, there + 128 : there + 256] = turned[64:128]
+
+
+def fill_outer(e):
+    for x, ring, tile in ((1, 0, 0), (4, 5, 2)):
+        there = TILE * (2 - tile)
+        for y in (0, 4):
+            turned = turn_dense(e, x, y, tile)
+            e[ring, y, :, there + 128 : there + 256] = turned[0:64]
+            e[ring, y + 1, :, there : there + 128] = turned[64:128]
+    for x in (2, 3, 4):
+        e[x, 0, :, 128:256] = turn_dense(e, x - 1, 0, 2)[0:64]
+        e[x, 5, :, 0:128] = turn_dense(e, x - 1, 4, 2)[64:128]
 
 
 def kernel(
@@ -115,6 +156,8 @@
     spread_strips(raw_h, e_h)
     for copy in copies_h:
         copy.start()
+    fill_inner(e_d)
+    fill_inner(e_h)
 
     hole = jnp.zeros((64, 128), jnp.bfloat16)
 
@@ -202,15 +245,19 @@
 
     for copy in copies_d:
         copy.wait_recv()
+    fill_outer(e_d)
     lax.fori_loop(0, 8, hp_body, 0)
     for copy in copies_h:
         copy.wait_recv()
+    fill_outer(e_h)
     lax.fori_loop(0, 8, sum_body, 0)
     for copy in copies_s:
         copy.start()
+    fill_inner(e_s)
     lax.fori_loop(0, 8, hpp_body, 0)
     for copy in copies_s:
         copy.wait_recv()
+    fill_outer(e_s)
     lax.fori_loop(0, 4, last_body, 0)
     for x in range(4):
         store(x).start()

time: 38.6 us -> 32.1 us (0.83)
  Pallas kernels: 35.9 us -> 29.4 us
    pallas_call x1, Pallas kernels: 35.9 us -> 29.4 us  [per_device(): pl.pallas_call(functools.partial(kernel, nx, ny), out_shape=jax.ShapeDtyp...]
where the time goes in v2:
time: 32.1 us; the launch traced here: 31.9 us
  Pallas kernels  29.4 us (92%)
  local copies, waits for them, and re-layouts  2.49 us (8%)
    pallas_call x1, Pallas kernels, per_device(): pl.pallas_call(functools.partial(kernel, nx, ny), out_shape=jax.ShapeDtyp...  29.4 us
    unnamed x1, local copies, waits for them, and re-layouts  2.49 us

profile of v2, /device:TPU:0, one launch (start us, length us, event | category | flops | bytes accessed | tf_op | source)
XLA Modules:
  0.0 31.9 jit_solution(16035051741880533901)
XLA Ops:
  0.0 29.4 %shard_map.46 = bf16[4,4,64,576]{3,2,1,0:T(8,128)(2,1)} custom-call(bf16[4,4,64,576]{3,2,1,0:T(8,128)(2,1)} %ham.1, bf16[4,4,64,576]{3,2,1,0:T(8,128)(2,1)} %den.1, s32[4,4,9]{2,1,0:T(4,128)} %pat.1, s32[4,4,9]{2,1,0:T(4,128)} %fil.1), custom_call_target="tpu_custom_call" | custom-call | tf_op jit(solution)/shard_map/pallas_call | solution.py:275
  29.4 2.5 %copy.6 = bf16[4,4,64,576]{3,2,1,0:T(8,128)(2,1)} copy(bf16[4,4,64,576]{3,2,1,0:T(8,128)(2,1)} %shard_map.46) | data formatting | bytes 2359296

commit v3 on v2

--- a/solution.py
+++ b/solution.py
@@ -125,7 +125,7 @@
             e[x + 1, 2 * p + 2, :, 512:768] = v[:, 320:576] * m[:, 512:768]
             return carry
 
-        lax.fori_loop(0, 8, body, 0)
+        lax.fori_loop(0, 8, body, 0, unroll=8)
 
     def copies(e, base):
         made = []
@@ -246,20 +246,20 @@
     for copy in copies_d:
         copy.wait_recv()
     fill_outer(e_d)
-    lax.fori_loop(0, 8, hp_body, 0)
+    lax.fori_loop(0, 8, hp_body, 0, unroll=8)
     for copy in copies_h:
         copy.wait_recv()
     fill_outer(e_h)
-    lax.fori_loop(0, 8, sum_body, 0)
+    lax.fori_loop(0, 8, sum_body, 0, unroll=8)
     for copy in copies_s:
         copy.start()
     fill_inner(e_s)
-    lax.fori_loop(0, 8, hpp_body, 0)
+    lax.fori_loop(0, 8, hpp_body, 0, unroll=8)
     for copy in copies_s:
         copy.wait_recv()
     fill_outer(e_s)
-    lax.fori_loop(0, 4, last_body, 0)
     for x in range(4):
+        last_body(x, 0)
         store(x).start()
     for copy in copies_d + copies_h + copies_s:
         copy.wait_send()

time: 32.1 us -> 29 us (0.903)
  Pallas kernels: 29.4 us -> 26.3 us
    pallas_call x1, Pallas kernels: 29.4 us -> 26.3 us  [per_device(): pl.pallas_call(functools.partial(kernel, nx, ny), out_shape=jax.ShapeDtyp...]
where the time goes in v3:
time: 29 us; the launch traced here: 28.8 us
  Pallas kernels  26.3 us (91%)
  local copies, waits for them, and re-layouts  2.49 us (9%)
    pallas_call x1, Pallas kernels, per_device(): pl.pallas_call(functools.partial(kernel, nx, ny), out_shape=jax.ShapeDtyp...  26.3 us
    unnamed x1, local copies, waits for them, and re-layouts  2.49 us

profile of v3, /device:TPU:0, one launch (start us, length us, event | category | flops | bytes accessed | tf_op | source)
XLA Modules:
  0.0 28.8 jit_solution(8724492138788090313)
XLA Ops:
  0.0 26.3 %shard_map.46 = bf16[4,4,64,576]{3,2,1,0:T(8,128)(2,1)} custom-call(bf16[4,4,64,576]{3,2,1,0:T(8,128)(2,1)} %ham.1, bf16[4,4,64,576]{3,2,1,0:T(8,128)(2,1)} %den.1, s32[4,4,9]{2,1,0:T(4,128)} %pat.1, s32[4,4,9]{2,1,0:T(4,128)} %fil.1), custom_call_target="tpu_custom_call" | custom-call | tf_op jit(solution)/shard_map/pallas_call | solution.py:275
  26.3 2.5 %copy.6 = bf16[4,4,64,576]{3,2,1,0:T(8,128)(2,1)} copy(bf16[4,4,64,576]{3,2,1,0:T(8,128)(2,1)} %shard_map.46) | data formatting | bytes 2359296

commit v4 on v3

--- a/solution.py
+++ b/solution.py
@@ -21,23 +21,26 @@
     to_y = {1: pl.ds(0, 1), -1: pl.ds(5, 1), 0: pl.ds(1, 4)}[sy]
     half = 128 if sy == 1 else 0
     if sy == 0:
-        parts = [(from_x, to_x, TILE, TILE)]
+        rows = (pl.ds(1, 4), pl.ds(2, 1), pl.ds(4, 1))
+        parts = [(from_x, to_x, y, y, TILE + (128 if i else 0)) for i, y in enumerate(rows)]
     elif sx != 0:
-        parts = [(from_x, to_x, TILE + half, 128)]
+        parts = [(from_x, to_x, from_y, to_y, TILE + half)]
     else:
-        first = pl.ds(1, 1)
-        parts = [
-            (first, first, half, 128),
-            (from_x, to_x, 2 * TILE + half, 128),
-            (from_x, to_x, TILE + half, 128),
-        ]
+        ends = ((pl.ds(1, 1), half), (pl.ds(4, 1), 2 * TILE + half))
+        parts = [(x, x, from_y, to_y, start) for x, start in ends]
     return [
-        ((a, from_y, whole, pl.ds(start, size)), (b, to_y, whole, pl.ds(start, size)))
-        for a, b, start, size in parts
+        ((a, c, whole, pl.ds(start, 128)), (b, d, whole, pl.ds(start, 128)))
+        for a, b, c, d, start in parts
     ]
 
 
-COPIES = sum(len(halo_parts(sx, sy)) for sx, sy in SIDES)
+COPIES = sum(len(halo_parts(sx, sy)) for sx, sy in SIDES) + 2
+
+
+def pack(e, packed):
+    for x in range(4):
+        packed[0, x] = jnp.concatenate([e[x + 1, 4, :, 384:448], e[x + 1, 4, :, 640:704]], axis=1)
+        packed[1, x] = jnp.concatenate([e[x + 1, 1, :, 320:384], e[x + 1, 1, :, 576:640]], axis=1)
 
 
 def turn_dense(e, x, y, tile):
@@ -61,7 +64,28 @@
             e[ring, y - 1, :, there + 128 : there + 256] = turned[64:128]
 
 
-def fill_outer(e):
+    gap = jnp.zeros((64, 128), jnp.bfloat16)
+    for x in (1, 2, 3, 4):
+        for step in (0, 1) if x < 4 else (0,):
+            there, here = TILE * (1 + step), TILE * (1 - step)
+            pile = jnp.concatenate([gap, e[x + step, 1, :, here : here + 128]], axis=0)
+            e[x, 0, :, there + 128 : there + 256] = pile.T[0:64]
+            pile = jnp.concatenate([e[x + step, 4, :, here + 128 : here + 256], gap], axis=0)
+            e[x, 5, :, there : there + 128] = pile.T[64:128]
+
+
+def fill_outer(e, packed):
+    gap = jnp.zeros((64, 128), jnp.bfloat16)
+    for x in (1, 2, 3, 4):
+        e[x, 0, :, 384:448] = packed[0, x - 1, :, 0:64]
+        e[x, 5, :, 320:384] = packed[1, x - 1, :, 0:64]
+        if x < 4:
+            e[x, 0, :, 640:704] = packed[0, x - 1, :, 64:128]
+            e[x, 5, :, 576:640] = packed[1, x - 1, :, 64:128]
+    for ring in (0, 5):
+        for y in (1, 3):
+            pile = jnp.concatenate([e[ring, y + 1, :, 256:384], gap], axis=0)
+            e[ring, y, :, 384:512] = pile.T[64:128]
     for x, ring, tile in ((1, 0, 0), (4, 5, 2)):
         there = TILE * (2 - tile)
         for y in (0, 4):
@@ -75,7 +99,7 @@
 
 def kernel(
     nx, ny, ham, den, pat, fil, out,
-    raw_h, raw_d, pat_row, fil_row, e_h, e_d, e_s, hp, total, result,
+    raw_h, raw_d, pat_row, fil_row, e_h, e_d, e_s, hp, total, result, packs, unpacks,
     load_sem, store_sem, send_sem, recv_sem,
 ):
     gx = lax.axis_index("gx")
@@ -127,14 +151,19 @@
 
         lax.fori_loop(0, 8, body, 0, unroll=8)
 
-    def copies(e, base):
+    def copies(e, which):
+        base = COPIES * which
         made = []
         for sx, sy in SIDES:
-            for source, target in halo_parts(sx, sy):
+            parts = [(e.at[source], e.at[target]) for source, target in halo_parts(sx, sy)]
+            if sx == 0:
+                side = 0 if sy == 1 else 1
+                parts.append((packs.at[which, side], unpacks.at[which, side]))
+            for source, target in parts:
                 made.append(
                     pltpu.make_async_remote_copy(
-                        src_ref=e.at[source],
-                        dst_ref=e.at[target],
+                        src_ref=source,
+                        dst_ref=target,
                         send_sem=send_sem.at[base + len(made)],
                         recv_sem=recv_sem.at[base + len(made)],
                         device_id=device(sx, sy),
@@ -144,16 +173,18 @@
         return made
 
     copies_d = copies(e_d, 0)
-    copies_h = copies(e_h, COPIES)
-    copies_s = copies(e_s, 2 * COPIES)
+    copies_h = copies(e_h, 1)
+    copies_s = copies(e_s, 2)
 
     load_d.wait()
     spread_strips(raw_d, e_d)
+    pack(e_d, packs.at[0])
     pl.semaphore_wait(barrier, len(SIDES))
     for copy in copies_d:
         copy.start()
     load_h.wait()
     spread_strips(raw_h, e_h)
+    pack(e_h, packs.at[1])
     for copy in copies_h:
         copy.start()
     fill_inner(e_d)
@@ -245,19 +276,25 @@
 
     for copy in copies_d:
         copy.wait_recv()
-    fill_outer(e_d)
+    fill_outer(e_d, unpacks.at[0])
     lax.fori_loop(0, 8, hp_body, 0, unroll=8)
     for copy in copies_h:
         copy.wait_recv()
-    fill_outer(e_h)
-    lax.fori_loop(0, 8, sum_body, 0, unroll=8)
-    for copy in copies_s:
+    fill_outer(e_h, unpacks.at[1])
+    for step in (0, 1, 6, 7):
+        sum_body(step, 0)
+    for copy in copies_s[:4] + copies_s[10:]:
+        copy.start()
+    for step in (2, 3, 4, 5):
+        sum_body(step, 0)
+    pack(e_s, packs.at[2])
+    for copy in copies_s[4:10]:
         copy.start()
     fill_inner(e_s)
     lax.fori_loop(0, 8, hpp_body, 0, unroll=8)
     for copy in copies_s:
         copy.wait_recv()
-    fill_outer(e_s)
+    fill_outer(e_s, unpacks.at[2])
     for x in range(4):
         last_body(x, 0)
         store(x).start()
@@ -288,6 +325,8 @@
             pltpu.VMEM((4, 4, 64, LANES), jnp.bfloat16),
             pltpu.VMEM((4, 4, 64, LANES), jnp.float32),
             pltpu.VMEM(shape, jnp.bfloat16),
+            pltpu.VMEM((3, 2, 4, 64, 128), jnp.bfloat16),
+            pltpu.VMEM((3, 2, 4, 64, 128), jnp.bfloat16),
             pltpu.SemaphoreType.DMA((2,)),
             pltpu.SemaphoreType.DMA((4,)),
             pltpu.SemaphoreType.DMA((3 * COPIES,)),

time: 29 us -> 27 us (0.931)
  Pallas kernels: 26.3 us -> 24.3 us
    pallas_call x1, Pallas kernels: 26.3 us -> 24.3 us  [per_device(): pl.pallas_call(functools.partial(kernel, nx, ny), out_shape=jax.ShapeDtyp...]
where the time goes in v4:
time: 27 us; the launch traced here: 26.8 us
  Pallas kernels  24.3 us (90%)
  local copies, waits for them, and re-layouts  2.49 us (9%)
    pallas_call x1, Pallas kernels, per_device(): pl.pallas_call(functools.partial(kernel, nx, ny), out_shape=jax.ShapeDtyp...  24.3 us
    unnamed x1, local copies, waits for them, and re-layouts  2.49 us

profile of v4, /device:TPU:0, one launch (start us, length us, event | category | flops | bytes accessed | tf_op | source)
XLA Modules:
  0.0 26.8 jit_solution(2863195555387221505)
XLA Ops:
  0.0 24.3 %shard_map.46 = bf16[4,4,64,576]{3,2,1,0:T(8,128)(2,1)} custom-call(bf16[4,4,64,576]{3,2,1,0:T(8,128)(2,1)} %ham.1, bf16[4,4,64,576]{3,2,1,0:T(8,128)(2,1)} %den.1, s32[4,4,9]{2,1,0:T(4,128)} %pat.1, s32[4,4,9]{2,1,0:T(4,128)} %fil.1), custom_call_target="tpu_custom_call" | custom-call | tf_op jit(solution)/shard_map/pallas_call | solution.py:312
  24.3 2.5 %copy.6 = bf16[4,4,64,576]{3,2,1,0:T(8,128)(2,1)} copy(bf16[4,4,64,576]{3,2,1,0:T(8,128)(2,1)} %shard_map.46) | data formatting | bytes 2359296

commit v5 on v4

--- a/solution.py
+++ b/solution.py
@@ -99,8 +99,8 @@
 
 def kernel(
     nx, ny, ham, den, pat, fil, out,
-    raw_h, raw_d, pat_row, fil_row, e_h, e_d, e_s, hp, total, result, packs, unpacks,
-    load_sem, store_sem, send_sem, recv_sem,
+    raw_h, raw_d, pat_row, fil_row, e_h, e_d, e_s, hp, total, packs, unpacks,
+    load_sem, send_sem, recv_sem,
 ):
     gx = lax.axis_index("gx")
     gy = lax.axis_index("gy")
@@ -256,9 +256,6 @@
             )
         return carry
 
-    def store(x):
-        return pltpu.make_async_copy(result.at[x], out.at[x], store_sem.at[x])
-
     def last_body(x, carry):
         for p in range(2):
             left = e_d[x + 1, pl.ds(2 * p + 1, 2)]
@@ -268,8 +265,8 @@
                 value = product(left, e_s, x, p, target)
                 value = total[x, pl.ds(2 * p, 2), :, lanes].reshape(128, TILE) - 2.0 * value
                 parts.append((value * filter_of(x, p, target)).astype(jnp.bfloat16))
-            result[x, 2 * p] = jnp.concatenate([part[0:64, 0:192] for part in parts], axis=1)
-            result[x, 2 * p + 1] = jnp.concatenate(
+            out[x, 2 * p] = jnp.concatenate([part[0:64, 0:192] for part in parts], axis=1)
+            out[x, 2 * p + 1] = jnp.concatenate(
                 [part[64:128, 64:256] for part in parts], axis=1
             )
         return carry
@@ -297,11 +294,8 @@
     fill_outer(e_s, unpacks.at[2])
     for x in range(4):
         last_body(x, 0)
-        store(x).start()
     for copy in copies_d + copies_h + copies_s:
         copy.wait_send()
-    for x in range(4):
-        store(x).wait()
 
 
 def per_device(nx, ny, hamiltonian, density, block_pattern, filter_mask):
@@ -313,7 +307,7 @@
         functools.partial(kernel, nx, ny),
         out_shape=jax.ShapeDtypeStruct(shape, jnp.bfloat16),
         in_specs=[anywhere, anywhere, vmem, vmem],
-        out_specs=anywhere,
+        out_specs=vmem,
         scratch_shapes=[
             pltpu.VMEM(shape, jnp.bfloat16),
             pltpu.VMEM(shape, jnp.bfloat16),
@@ -324,15 +318,15 @@
             pltpu.VMEM(ring, jnp.bfloat16),
             pltpu.VMEM((4, 4, 64, LANES), jnp.bfloat16),
             pltpu.VMEM((4, 4, 64, LANES), jnp.float32),
-            pltpu.VMEM(shape, jnp.bfloat16),
             pltpu.VMEM((3, 2, 4, 64, 128), jnp.bfloat16),
             pltpu.VMEM((3, 2, 4, 64, 128), jnp.bfloat16),
             pltpu.SemaphoreType.DMA((2,)),
-            pltpu.SemaphoreType.DMA((4,)),
             pltpu.SemaphoreType.DMA((3 * COPIES,)),
             pltpu.SemaphoreType.DMA((3 * COPIES,)),
         ],
-        compiler_params=pltpu.CompilerParams(collective_id=0, has_side_effects=True),
+        compiler_params=pltpu.CompilerParams(
+            collective_id=0, has_side_effects=True, vmem_limit_bytes=53000 << 10
+        ),
     )(hamiltonian, density, block_pattern, filter_mask)
 
 

time: 27 us -> 25.6 us (0.948)
  Pallas kernels: 24.3 us -> 22.9 us
    pallas_call x1, Pallas kernels: 24.3 us -> 22.9 us  [per_device(): pl.pallas_call(functools.partial(kernel, nx, ny), out_shape=jax.ShapeDtyp...]
    unnamed x1 -> x5, local copies, waits for them, and re-layouts: 2.49 us -> 2.45 us
where the time goes in v5:
time: 25.6 us; the launch traced here: 25.4 us
  Pallas kernels  22.9 us (89%)
  local copies, waits for them, and re-layouts  2.45 us (10%)
    pallas_call x1, Pallas kernels, per_device(): pl.pallas_call(functools.partial(kernel, nx, ny), out_shape=jax.ShapeDtyp...  22.9 us
    unnamed x5, local copies, waits for them, and re-layouts  2.45 us

profile of v5, /device:TPU:0, one launch (start us, length us, event | category | flops | bytes accessed | tf_op | source)
XLA Modules:
  0.0 25.4 jit_solution(1080286328212639131)
XLA Ops:
  0.0 0.0 copy-start
  0.0 0.7 %copy-done = s32[4,4,9]{2,1,0:T(4,128)S(1)} copy-done((s32[4,4,9]{2,1,0:T(4,128)S(1)}, s32[4,4,9]{2,1,0:T(4,128)}, u32[]{:S(2)}) %copy-start) | copy-done | bytes 600
  0.7 0.0 copy-start.1
  0.7 0.7 %copy-done.1 = s32[4,4,9]{2,1,0:T(4,128)S(1)} copy-done((s32[4,4,9]{2,1,0:T(4,128)S(1)}, s32[4,4,9]{2,1,0:T(4,128)}, u32[]{:S(2)}) %copy-start.1) | copy-done | bytes 600
  1.4 22.9 %shard_map.46 = bf16[4,4,64,576]{3,2,1,0:T(8,128)(2,1)S(1)} custom-call(bf16[4,4,64,576]{3,2,1,0:T(8,128)(2,1)} %ham.1, bf16[4,4,64,576]{3,2,1,0:T(8,128)(2,1)} %den.1, s32[4,4,9]{2,1,0:T(4,128)S(1)} %copy-done, s32[4,4,9]{2,1,0:T(4,128)S(1)} %copy-done.1), custom_call_target="tpu_custom_call" | custom-call | tf_op jit(solution)/shard_map/pallas_call | solution.py:306
  24.3 1.1 %copy.6 = bf16[4,4,64,576]{3,2,1,0:T(8,128)(2,1)} copy(bf16[4,4,64,576]{3,2,1,0:T(8,128)(2,1)S(1)} %shard_map.46) | data formatting | bytes 2359296
Async XLA Ops:
  0.0 0.7 %copy-start = (s32[4,4,9]{2,1,0:T(4,128)S(1)}, s32[4,4,9]{2,1,0:T(4,128)}, u32[]{:S(2)}) copy-start(s32[4,4,9]{2,1,0:T(4,128)} %pat.1) | copy-start | bytes 1732
  0.7 0.7 %copy-start.1 = (s32[4,4,9]{2,1,0:T(4,128)S(1)}, s32[4,4,9]{2,1,0:T(4,128)}, u32[]{:S(2)}) copy-start(s32[4,4,9]{2,1,0:T(4,128)} %fil.1) | copy-start | bytes 1732
